TPU v7x, 32 devices: a whole 2x2x4 slice. The times are simulated.
32 devices in a mesh: seq: 8 (over z, x), hid: 4 (over y, core).
Axes of the slice: x: 2, y: 2, z: 4, core: 2. Of those that a mesh axis runs over, the one named last changes fastest.
Arguments:
- tokens: bfloat16 [1024, 4096], P('seq', 'hid'), may hold values from -6 to 6
- hidden_grad: bfloat16 [1024, 14336], P('seq', 'hid'), may hold values from -6 to 6
- gate_blocks: bfloat16 [4, 448, 128, 128], P('hid', 'seq'), may hold values from -0.125 to 0.125
- up_blocks: bfloat16 [4, 448, 128, 128], P('hid', 'seq'), may hold values from -0.125 to 0.125
- gate_rows: int32 [4, 448], P('hid'), may hold values from 0 to 31, as said below
- gate_cols: int32 [4, 448], P('hid'), may hold values from 0 to 27
- gate_count: int32 [4], P('hid'), may hold values from 56 to 448, as said below
- up_rows: int32 [4, 448], P('hid'), may hold values from 0 to 31, as said below
- up_cols: int32 [4, 448], P('hid'), may hold values from 0 to 27
- up_count: int32 [4], P('hid'), may hold values from 56 to 448, as said below
Outputs:
- hidden: bfloat16 [1024, 14336], P('seq', 'hid')
- input_grad: bfloat16 [1024, 4096], P('seq', 'hid')
- gate_block_grads: bfloat16 [4, 448, 128, 128], P('hid', 'seq')
- up_block_grads: bfloat16 [4, 448, 128, 128], P('hid', 'seq')
Inputs may be any that keep to these rules, and one draw needn't show every extreme that they name: For each panel, the pairs (gate_rows, gate_cols) over all 448 slots are distinct. `gate_count`: slots at or after a panel's count hold no block of the matrix. For each panel, the pairs (up_rows, up_cols) over all 448 slots are distinct. `up_count`: slots at or after a panel's count hold no block of the matrix.
All inputs are finite; a program needn't handle non-finite values.
Results may differ from a plain program's by a relative error of at most 0.018.
Values may be sent and summed in bfloat16 or wider, within the bound.
A program may use at most 192 MiB of HBM per device.

v0:
```python
import math
import jax
import jax.numpy as jnp
from jax import lax
from jax.sharding import PartitionSpec as P


def swapped(value, axis, stride):
    mask = 2**stride
    pairs = [(source, source ^ mask) for source in range(lax.axis_size(axis))]
    return lax.ppermute(value, axis, pairs)


def silu_parts(preact):
    sigma = jax.nn.sigmoid(preact)
    return (preact * sigma, sigma * (1.0 + preact * (1.0 - sigma)))


def place_split(products, placing, form):
    high_part = products.astype(jnp.bfloat16)
    rest_part = (products - high_part.astype(jnp.float32)).astype(jnp.bfloat16)
    table = placing.astype(jnp.bfloat16)
    placed = jnp.einsum(form, high_part, table, preferred_element_type=jnp.float32)
    return placed + jnp.einsum(form, rest_part, table, preferred_element_type=jnp.float32)


def project_slots(tiles, weights, rows, columns, live_count, group_size, trips, col_blocks):
    tok_rows = tiles.shape[0]
    block_size = tiles.shape[2]
    targets = jnp.arange(col_blocks)
    offsets = jnp.arange(group_size)

    def project_one_group(group_index, running):
        start = group_index * group_size
        chosen = lax.dynamic_slice_in_dim(weights, start, group_size, 0)
        row_ids = lax.dynamic_slice_in_dim(rows, start, group_size, 0)
        col_ids = lax.dynamic_slice_in_dim(columns, start, group_size, 0)
        active = start + offsets < live_count
        picked = jnp.take(tiles, row_ids, axis=1)
        products = jnp.einsum("tsk,skn->tsn", picked, chosen, preferred_element_type=jnp.float32)
        placing = (col_ids[:, None] == targets[None, :]) & active[:, None]
        return running + place_split(products, placing, "tsn,sc->tcn")

    initial = jnp.zeros((tok_rows, col_blocks, block_size), jnp.float32)
    return lax.fori_loop(0, trips, project_one_group, initial)


def return_slots(grad_tiles, weights, rows, columns, live_count, group_size, trips, row_blocks):
    tok_rows = grad_tiles.shape[0]
    block_size = grad_tiles.shape[2]
    targets = jnp.arange(row_blocks)
    offsets = jnp.arange(group_size)

    def return_one_group(group_index, running):
        start = group_index * group_size
        chosen = lax.dynamic_slice_in_dim(weights, start, group_size, 0)
        row_ids = lax.dynamic_slice_in_dim(rows, start, group_size, 0)
        col_ids = lax.dynamic_slice_in_dim(columns, start, group_size, 0)
        active = start + offsets < live_count
        picked = jnp.take(grad_tiles, col_ids, axis=1)
        products = jnp.einsum("tsn,skn->tsk", picked, chosen, preferred_element_type=jnp.float32)
        placing = (row_ids[:, None] == targets[None, :]) & active[:, None]
        return running + place_split(products, placing, "tsk,sr->trk")

    initial = jnp.zeros((tok_rows, row_blocks, block_size), jnp.float32)
    return lax.fori_loop(0, trips, return_one_group, initial)


def on_device(
    tokens,
    hidden_grad,
    gate_blocks,
    up_blocks,
    gate_rows,
    gate_cols,
    gate_count,
    up_rows,
    up_cols,
    up_count,
):
    gathered = lax.all_gather(tokens, "hid", axis=1, tiled=True)
    tok_rows = gathered.shape[0]
    block_size = gate_blocks.shape[2]
    row_blocks = gathered.shape[1] // block_size
    col_blocks = hidden_grad.shape[1] // block_size
    gate_all = lax.all_gather(gate_blocks, "seq", axis=1, tiled=True)
    up_all = lax.all_gather(up_blocks, "seq", axis=1, tiled=True)
    capacity = gate_all.shape[1]
    group_size = 32
    groups = capacity // group_size
    gate_live = gate_count[0]
    up_live = up_count[0]
    tiles = gathered.reshape(tok_rows, row_blocks, block_size)
    gate_pre = project_slots(
        tiles, gate_all[0], gate_rows[0], gate_cols[0], gate_live, group_size, groups, col_blocks
    )
    up_pre = project_slots(
        tiles, up_all[0], up_rows[0], up_cols[0], up_live, group_size, groups, col_blocks
    )
    activated, slope = silu_parts(gate_pre)
    hidden = (activated * up_pre).astype(jnp.bfloat16)
    upstream = hidden_grad.reshape(tok_rows, col_blocks, block_size).astype(jnp.float32)
    gate_grad = (upstream * up_pre * slope).astype(jnp.bfloat16)
    up_grad = (upstream * activated).astype(jnp.bfloat16)
    input_sum = return_slots(
        gate_grad,
        gate_all[0],
        gate_rows[0],
        gate_cols[0],
        gate_live,
        group_size,
        groups,
        row_blocks,
    )
    input_sum = input_sum + return_slots(
        up_grad, up_all[0], up_rows[0], up_cols[0], up_live, group_size, groups, row_blocks
    )
    input_grad = lax.psum_scatter(
        input_sum.reshape(tok_rows, row_blocks * block_size).astype(jnp.bfloat16),
        "hid",
        scatter_dimension=1,
        tiled=True,
    )
    seq_count = lax.axis_size("seq")
    position = lax.axis_index("seq")
    levels = seq_count.bit_length() - 1
    blk_dev = capacity // seq_count
    other_tiles, other_gate, other_up = swapped((tiles, gate_grad, up_grad), "seq", 0)
    both_tiles = jnp.concatenate([tiles, other_tiles], axis=0)
    both_gate = jnp.concatenate([gate_grad, other_gate], axis=0)
    both_up = jnp.concatenate([up_grad, other_up], axis=0)
    parity = position % 2
    owners = 2 * jnp.arange(seq_count // 2) + parity
    slot_ids = (owners[:, None] * blk_dev + jnp.arange(blk_dev)[None, :]).reshape(-1)
    stacked = []
    for rows, columns, live_count, grad_tiles in (
        (gate_rows[0], gate_cols[0], gate_live, both_gate),
        (up_rows[0], up_cols[0], up_live, both_up),
    ):
        row_ids = jnp.take(rows, slot_ids)
        col_ids = jnp.take(columns, slot_ids)
        picked_input = jnp.take(both_tiles, row_ids, axis=1)
        picked_grad = jnp.take(grad_tiles, col_ids, axis=1)
        block_term = jnp.einsum(
            "tsk,tsn->skn", picked_input, picked_grad, preferred_element_type=jnp.float32
        )
        stacked.append(block_term * (slot_ids < live_count).astype(jnp.float32)[:, None, None])
    current = jnp.stack(stacked, axis=1)
    current = current.reshape((seq_count // 2, blk_dev) + current.shape[1:])
    for level in range(1, levels):
        own_bit = position // 2**level % 2
        halves = current.reshape((current.shape[0] // 2, 2) + current.shape[1:])
        kept = lax.dynamic_index_in_dim(halves, own_bit, 1, keepdims=False)
        sent = lax.dynamic_index_in_dim(halves, 1 - own_bit, 1, keepdims=False)
        received = swapped(sent.astype(jnp.bfloat16), "seq", level)
        current = kept + received.astype(jnp.float32)
    summed = current[0]
    scale = 1.0 / math.sqrt(tok_rows * seq_count)
    gate_block_grads = (summed[:, 0] * scale).astype(jnp.bfloat16)[None]
    up_block_grads = (summed[:, 1] * scale).astype(jnp.bfloat16)[None]
    return (
        hidden.reshape(tok_rows, col_blocks * block_size),
        input_grad,
        gate_block_grads,
        up_block_grads,
    )


def solution(mesh):
    placed = (
        P("seq", "hid"),
        P("seq", "hid"),
        P("hid", "seq", None, None),
        P("hid", "seq", None, None),
        P("hid", None),
        P("hid", None),
        P("hid"),
        P("hid", None),
        P("hid", None),
        P("hid"),
    )
    return jax.shard_map(
        on_device,
        mesh=mesh,
        in_specs=placed,
        out_specs=(
            P("seq", "hid"),
            P("seq", "hid"),
            P("hid", "seq", None, None),
            P("hid", "seq", None, None),
        ),
        check_vma=False,
    )
```

profile of v0, /device:TPU:0, one launch (start us, length us, event | category | flops | bytes accessed | tf_op | source)
XLA Modules:
  0.0 1165.3 jit_solution(1844786483724718215)
XLA Ops:
  16.3 13.3 %all-gather.6.cloned.1.call-done = bf16[128,4096]{0,1:T(8,128)(2,1)} async-done(((bf16[128,1024]{0,1:T(8,128)(2,1)}), bf16[128,4096]{0,1:T(8,128)(2,1)}) %all-gather.6.cloned.1.call-update) | async-done | bytes 1048592 | tf_op jit(solution)/shard_map/all_gather | solution.py:81
  33.3 200.2 %all-gather.8.cloned.1.call-done = bf16[1,448,128,128]{3,2,0,1:T(8,128)(2,1)} async-done(((bf16[1,56,128,128]{3,2,0,1:T(8,128)(2,1)}), bf16[1,448,128,128]{3,2,0,1:T(8,128)(2,1)}) %all-gather.8.cloned.1.call-update) | async-done | bytes 14680080 | tf_op jit(solution)/shard_map/all_gather | solution.py:87
  233.5 192.3 %while.61 = (s32[]{:T(128)}, f32[128,28,128]{2,1,0:T(8,128)}, s32[448]{0:T(512)S(1)}, s32[]{:T(128)}, bf16[448,128,128]{2,1,0:T(8,128)(2,1)}, /*index=5*/s32[448...) while((s32[]{:T(128)}, f32[128,28,128]{2,1,0:T(8,128)}, ...), condition=%wide.region_3.5_spmd.clone, body=%wide.region_2.4_spmd.clone.sunk | while | flops 196940544 | bytes 19928416 | solution.py:45
  311.5 4.6 bitcast_add_fusion.9
  394.6 3.9 bitcast_add_fusion.9
  425.8 9.8 all-gather.4.cloned.1.call-done
  435.6 193.2 %while.60 = (s32[]{:T(128)}, f32[128,28,128]{2,1,0:T(8,128)}, s32[448]{0:T(512)S(1)}, s32[]{:T(128)}, bf16[448,128,128]{2,1,0:T(8,128)(2,1)}, /*index=5*/s32[448...) while((s32[]{:T(128)}, f32[128,28,128]{2,1,0:T(8,128)}, ...), condition=%wide.region_1.3_spmd.clone, body=%wide.region_0.2_spmd.clone.sunk | while | flops 196940544 | bytes 19928416 | solution.py:45
  569.6 3.8 bitcast_add_fusion.8
  628.8 6.5 multiply_convert_fusion.1
  645.1 9.4 gather_fusion.5
  654.5 9.2 gather_fusion.9
  665.3 9.2 gather_fusion.7
  678.0 9.1 gather_fusion.11
  687.2 18.4 %fusion.105 = f32[224,128,128]{2,1,0:T(8,128)} fusion(bf16[224,256,128]{2,1,0:T(8,128)(2,1)} %gather_fusion.7, pred[224]{0:T(512)(128)(4,1)S(1)} %get-tuple-element.961, bf16[224,256,128]{2,1,0:T(8,128)(2,1)} %gather_fusion.5, pred[224]{0:T(512)(128)(4,1)S(1)} %get-tuple-element.963, f32[224]{0:T(256)S(1)} %get-tuple-element.960), kind=kOutput, calls=%fused_computation.141 | convolution fusion | flops 1897398272 | bytes 44041536 | tf_op jit(solution)/shard_map/tsk,tsn->skn/dot_general | solution.py:144
  705.6 18.5 %fusion.110 = f32[224,128,128]{2,1,0:T(8,128)} fusion(bf16[224,256,128]{2,1,0:T(8,128)(2,1)} %gather_fusion.11, pred[224]{0:T(512)(128)(4,1)S(1)} %get-tuple-element.944, bf16[224,256,128]{2,1,0:T(8,128)(2,1)} %gather_fusion.9, pred[224]{0:T(512)(128)(4,1)S(1)} %get-tuple-element.941, f32[224]{0:T(256)S(1)} %get-tuple-element.959), kind=kOutput, calls=%fused_computation.142 | convolution fusion | flops 1897398272 | bytes 44041536 | tf_op jit(solution)/shard_map/tsk,tsn->skn/dot_general | solution.py:144
  724.1 10.1 fusion.115
  734.2 192.1 %while.62 = (s32[]{:T(128)}, f32[128,32,128]{2,1,0:T(8,128)}, s32[448]{0:T(512)S(1)}, s32[]{:T(128)}, bf16[448,128,128]{2,1,0:T(8,128)(2,1)}, /*index=5*/s32[448...) while((s32[]{:T(128)}, f32[128,32,128]{2,1,0:T(8,128)}, ...), condition=%wide.region_5.8_spmd.clone.clone, body=%wide.region_4.0_spmd.clone.clone.sunk | while | flops 205526272 | bytes 20976992 | solution.py:66
  757.1 3.9 bitcast_add_fusion.10
  770.9 3.9 bitcast_add_fusion.10
  784.7 3.9 bitcast_add_fusion.10
  798.5 3.9 bitcast_add_fusion.10
  812.2 3.9 bitcast_add_fusion.10
  826.0 3.9 bitcast_add_fusion.10
  839.8 3.9 bitcast_add_fusion.10
  853.5 3.9 bitcast_add_fusion.10
  867.3 3.9 bitcast_add_fusion.10
  881.1 3.9 bitcast_add_fusion.10
  894.8 3.9 bitcast_add_fusion.10
  908.6 3.9 bitcast_add_fusion.10
  922.4 3.9 bitcast_add_fusion.10
  926.2 8.6 fusion.90
  934.9 5.1 copy-done.7
  945.5 186.0 %while.63 = (s32[]{:T(128)}, f32[128,32,128]{2,1,0:T(8,128)}, s32[448]{0:T(512)}, s32[]{:T(128)}, bf16[448,128,128]{2,1,0:T(8,128)(2,1)}, /*index=5*/s32[448]{0:...) while((s32[]{:T(128)}, f32[128,32,128]{2,1,0:T(8,128)}, ...), condition=%wide.region_7.10_spmd.clone.clone, body=%wide.region_6.9_spmd.clone.clone.sunk | while | flops 205526272 | bytes 24647044 | solution.py:66
  967.5 3.9 bitcast_add_fusion.11
  980.9 3.9 bitcast_add_fusion.11
  994.2 3.9 bitcast_add_fusion.11
  1007.5 3.9 bitcast_add_fusion.11
  1020.9 3.9 bitcast_add_fusion.11
  1034.2 3.9 bitcast_add_fusion.11
  1047.5 3.9 bitcast_add_fusion.11
  1060.8 3.9 bitcast_add_fusion.11
  1074.2 3.9 bitcast_add_fusion.11
  1087.5 3.9 bitcast_add_fusion.11
  1100.8 3.9 bitcast_add_fusion.11
  1114.2 3.9 bitcast_add_fusion.11
  1127.5 3.9 bitcast_add_fusion.11
  1137.6 5.8 add_bitcast_fusion
  1146.2 12.6 %reduce-scatter.2.cloned.1.call-done = bf16[128,1024]{1,0:T(8,128)(2,1)} async-done(((bf16[128,4096]{1,0:T(8,128)(2,1)}), bf16[128,1024]{1,0:T(8,128)(2,1)}) %reduce-scatter.2.cloned.1.call-update) | async-done | bytes 262160 | tf_op jit(solution)/shard_map/reduce_scatter | solution.py:118
  (569 shorter events, 689.1 us)
Async XLA Ops:
  7.2 22.4 %all-gather.6.cloned.1.call-start = ((), (), s32[]{:S(2)}) async-start(), calls=%async_computation.2 | async-start | bytes 1310720 | tf_op jit(solution)/shard_map/all_gather | solution.py:81
  9.0 1.6 copy-start.9
  9.0 224.4 %all-gather.8.cloned.1.call-start = ((), (), s32[]{:S(2)}) async-start(), calls=%async_computation.3 | async-start | bytes 16515072 | tf_op jit(solution)/shard_map/all_gather | solution.py:87
  9.8 425.8 %all-gather.4.cloned.1.call-start = ((), (), s32[]{:S(2)}) async-start(), calls=%async_computation.1 | async-start | bytes 16515072 | tf_op jit(solution)/shard_map/all_gather | solution.py:86
  10.5 1148.3 %reduce-scatter.2.cloned.1.call-start = ((), (), s32[]{:S(2)}) async-start(), calls=%async_computation.4 | async-start | bytes 1310720 | tf_op jit(solution)/shard_map/reduce_scatter | solution.py:118
  10.6 3.7 copy-start.3
  12.8 220.6 %copy-start.2 = (s32[1,448]{1,0:T(1,128)S(1)}, s32[1,448]{1,0:T(1,128)}, u32[]{:S(2)}) copy-start(s32[1,448]{1,0:T(1,128)} %param.36) | copy-start | bytes 5380
  31.8 611.6 %collective-permute-start = (bf16[128,32,128]{2,0,1:T(8,128)(2,1)}, bf16[128,32,128]{2,0,1:T(8,128)(2,1)}, u32[]{:S(2)}, u32[]{:S(2)}) collective-permute-start(bf16[128,32,128]{2,0,1:T(8,128)(2,1)} %copy.98), channel_id=1, source_target_pairs={{0,4},{4,0},{8,12},{12,8},{16,20},{20,16},{24,28},{28,24},{1,5},{5... | collective-permute-start | bytes 3145736 | tf_op jit(solution)/shard_map/ppermute | solution.py:11
  233.5 202.1 %copy-start = (s32[1,448]{1,0:T(1,128)S(1)}, s32[1,448]{1,0:T(1,128)}, u32[]{:S(2)}) copy-start(s32[1,448]{1,0:T(1,128)} %param.33) | copy-start | bytes 5380
  233.5 202.1 %copy-start.1 = (s32[1,448]{1,0:T(1,128)S(1)}, s32[1,448]{1,0:T(1,128)}, u32[]{:S(2)}) copy-start(s32[1,448]{1,0:T(1,128)} %param.32) | copy-start | bytes 5380
  635.3 41.4 %copy-start.4 = (bf16[128,28,128]{2,0,1:T(8,128)(2,1)}, bf16[128,28,128]{2,0,1:T(8,128)(2,1)S(1)}, u32[]{:S(2)}) copy-start(bf16[128,28,128]{2,0,1:T(8,128)(2,1)S(1)} %get-tuple-element.1284) | copy-start | bytes 2752516
  635.3 28.4 %collective-permute-start.1 = (bf16[128,28,128]{2,0,1:T(8,128)(2,1)}, bf16[128,28,128]{2,0,1:T(8,128)(2,1)}, u32[]{:S(2)}, u32[]{:S(2)}) collective-permute-start(bf16[128,28,128]{2,0,1:T(8,128)(2,1)} %get-tuple-element.1251), channel_id=1, source_target_pairs={{0,4},{4,0},{8,12},{12,8},{16,20},{20,16},{24,28},{28,24},{1,5},{5... | collective-permute-start | bytes 2752520 | tf_op jit(solution)/shard_map/ppermute | solution.py:11
  635.9 40.8 %collective-permute-start.2 = (bf16[128,28,128]{2,0,1:T(8,128)(2,1)S(1)}, bf16[128,28,128]{2,0,1:T(8,128)(2,1)}, u32[]{:S(2)}, u32[]{:S(2)}) collective-permute-start(bf16[128,28,128]{2,0,1:T(8,128)(2,1)S(1)} %get-tuple-element.1284), channel_id=1, source_target_pairs={{0,4},{4,0},{8,12},{12,8},{16,20},{20,16},{24,28},{28,24},{1,5},{5... | collective-permute-start | bytes 2752520 | tf_op jit(solution)/shard_map/ppermute | solution.py:11
  734.2 192.1 %collective-permute-start.3 = (bf16[2,56,2,128,128]{4,3,1,2,0:T(8,128)(2,1)}, bf16[2,56,2,128,128]{4,3,1,2,0:T(8,128)(2,1)}, u32[]{:S(2)}, u32[]{:S(2)}) collective-permute-start(bf16[2,56,2,128,128]{4,3,1,2,0:T(8,128)(2,1)} %fusion.115), channel_id=1, source_target_pairs={{0,8},{4,12},{8,0},{12,4},{16,24},{20,28},{24,16},{28,20},{1,9},{5... | collective-permute-start | bytes 22020104 | tf_op jit(solution)/shard_map/ppermute | solution.py:11
  934.9 5.1 copy-start.7
  940.0 5.5 copy-start.5
  942.7 194.9 %collective-permute-start.4 = (bf16[1,56,2,128,128]{4,3,1,2,0:T(8,128)(2,1)}, bf16[1,56,2,128,128]{4,3,1,2,0:T(8,128)(2,1)}, u32[]{:S(2)}, u32[]{:S(2)}) collective-permute-start(bf16[1,56,2,128,128]{4,3,1,2,0:T(8,128)(2,1)} %dynamic-slice_convert_fusion), channel_id=1, source_target_pairs={{0,16},{4,20},{8,24},{12,28},{16,0},{20,4},{24,8},{28,12},{1,17},{... | collective-permute-start | bytes 11010056 | tf_op jit(solution)/shard_map/ppermute | solution.py:11
  954.9 3.3 copy-start.6
  967.5 3.9 copy-start.6
  980.9 3.9 copy-start.6
  994.2 3.9 copy-start.6
  1007.5 3.9 copy-start.6
  1020.9 3.9 copy-start.6
  1034.2 3.9 copy-start.6
  1047.5 3.9 copy-start.6
  1060.8 3.9 copy-start.6
  1074.2 3.9 copy-start.6
  1087.5 3.9 copy-start.6
  1100.8 3.9 copy-start.6
  1114.2 3.9 copy-start.6
  1127.5 3.9 copy-start.6
  1134.1 1.5 copy-start.8
Sparse Core Ops, SparseCore 0:
  10.1 19.4 all-gather.5
  31.8 201.6 all-gather.7
  235.7 199.8 all-gather.3
  1135.7 23.0 reduce-scatter.1
where the time goes:
time: 1170 us
  matrix products  462 us (39%)
  local copies, waits for them, and re-layouts  359 us (31%)
  waiting for transfers between devices  239 us (20%)
  other arithmetic  82.2 us (7%)
  between operations  15.4 us (1%)
    dot_general x56, matrix products, place_split(): jnp.einsum(form, rest_part, table, preferred_element_type=jnp.float32)  213 us
    all_gather x1, waiting for transfers between devices, on_device(): up_all = lax.all_gather(up_blocks, 'seq', axis=1, tiled=True)  200 us
    convert_element_type x56, local copies, waits for them, and re-layouts, place_split(): rest_part = (products - high_part.astype(jnp.float32)).astype(jnp.bfloat16)  95.1 us
    convert_element_type x56, local copies, waits for them, and re-layouts, place_split(): high_part = products.astype(jnp.bfloat16)  95 us
    dot_general x56, matrix products, place_split(): jnp.einsum(form, high_part, table, preferred_element_type=jnp.float32)  91.5 us
    dot_general x28, matrix products, return_one_group(): jnp.einsum('tsn,skn->tsk', picked, chosen, preferred_element_type=jnp.flo...  60.6 us
    dot_general x28, matrix products, project_one_group(): jnp.einsum('tsk,skn->tsn', picked, chosen, preferred_element_type=jnp.flo...  59.6 us
    gather x28, local copies, waits for them, and re-layouts, project_one_group(): picked = jnp.take(tiles, row_ids, axis=1)  55.3 us
  transfers between devices with their start and end apart: 9, of which 5 were waited for; matrix products, arithmetic and copies ran while one was open for 71% of the time, Pallas kernels for 0%

commit v1 on v0

--- a/solution.py
+++ b/solution.py
@@ -84,7 +84,16 @@
     row_blocks = gathered.shape[1] // block_size
     col_blocks = hidden_grad.shape[1] // block_size
     gate_all = lax.all_gather(gate_blocks, "seq", axis=1, tiled=True)
-    up_all = lax.all_gather(up_blocks, "seq", axis=1, tiled=True)
+    state_next = jax.lax.axis_size("seq")
+    base_arr = jax.lax.axis_index("seq")
+    low, k_now = (state_next, base_arr)
+    up_all, part_now = (up_blocks, 1)
+    while part_now < low:
+        val = jax.lax.ppermute(up_all, "seq", [(k0, k0 ^ part_now) for k0 in range(low)])
+        b_now = jnp.concatenate([up_all, val], axis=1)
+        block_out = jnp.concatenate([val, up_all], axis=1)
+        up_all = jnp.where(k_now & part_now == 0, b_now, block_out)
+        part_now = 2 * part_now
     capacity = gate_all.shape[1]
     group_size = 32
     groups = capacity // group_size

time: 1170 us -> 1590 us (1.36)
  waiting for transfers between devices: 239 us -> 606 us
  other arithmetic: 82.2 us -> 117 us
    ppermute x0 -> x3, waiting for transfers between devices: none -> 591 us  [on_device(): jax.lax.ppermute(up_all, 'seq', [(k0, k0 ^ part_now) for k0 in range(low)])]
    all_gather x1 -> x0, waiting for transfers between devices: 200 us -> none  [on_device(): up_all = lax.all_gather(up_blocks, 'seq', axis=1, tiled=True)]
    select_n x0 -> x5, other arithmetic: none -> 34.4 us  [on_device(): up_all = jnp.where(k_now & part_now == 0, b_now, block_out)]
  transfers between devices with their start and end apart: 9 -> 11, of which waited for: 5 -> 5; matrix products, arithmetic and copies ran while one was open for 71% -> 54% of each run, Pallas kernels for 0% -> 0%
where the time goes in v1:
time: 1590 us; the launch traced here: 1570 us
  waiting for transfers between devices  606 us (38%)
  matrix products  460 us (29%)
  local copies, waits for them, and re-layouts  356 us (22%)
  other arithmetic  117 us (7%)
    ppermute x3, waiting for transfers between devices, on_device(): jax.lax.ppermute(up_all, 'seq', [(k0, k0 ^ part_now) for k0 in range(low)])  591 us
    dot_general x56, matrix products, place_split(): jnp.einsum(form, rest_part, table, preferred_element_type=jnp.float32)  211 us
    convert_element_type x56, local copies, waits for them, and re-layouts, place_split(): rest_part = (products - high_part.astype(jnp.float32)).astype(jnp.bfloat16)  94.2 us
    convert_element_type x56, local copies, waits for them, and re-layouts, place_split(): high_part = products.astype(jnp.bfloat16)  94.2 us
    dot_general x56, matrix products, place_split(): jnp.einsum(form, high_part, table, preferred_element_type=jnp.float32)  91.4 us
    dot_general x28, matrix products, return_one_group(): jnp.einsum('tsn,skn->tsk', picked, chosen, preferred_element_type=jnp.flo...  60.7 us
    dot_general x28, matrix products, project_one_group(): jnp.einsum('tsk,skn->tsn', picked, chosen, preferred_element_type=jnp.flo...  59.5 us
    gather x28, local copies, waits for them, and re-layouts, project_one_group(): picked = jnp.take(tiles, row_ids, axis=1)  55.3 us
  transfers between devices with their start and end apart: 11, of which 5 were waited for; matrix products, arithmetic and copies ran while one was open for 54% of the time, Pallas kernels for 0%

profile of v1, /device:TPU:0, one launch (start us, length us, event | category | flops | bytes accessed | tf_op | source)
XLA Modules:
  0.0 1572.4 jit_solution(13205571290445734023)
XLA Ops:
  10.2 40.3 %collective-permute-done = bf16[1,56,128,128]{3,2,1,0:T(8,128)(2,1)} collective-permute-done((bf16[1,56,128,128]{3,2,1,0:T(8,128)(2,1)}, bf16[1,56,128,128]{3,2,1,0:T(8,128)(2,1)}, u32[]{:S(2)}, u32[]{:S(2)}) %collective-permute-start) | collective-permute-done | bytes 1835040 | tf_op jit(solution)/shard_map/ppermute | solution.py:92
  50.6 4.8 maximum_select_fusion.4
  60.5 75.6 %collective-permute-done.1 = bf16[1,112,128,128]{3,2,1,0:T(8,128)(2,1)} collective-permute-done((bf16[1,112,128,128]{3,2,1,0:T(8,128)(2,1)}, bf16[1,112,128,128]{3,2,1,0:T(8,128)(2,1)}, u32[]{:S(2)}, u32[]{:S(2)}) %collective-permute-start.1) | collective-permute-done | bytes 3670048 | tf_op jit(solution)/shard_map/ppermute | solution.py:92
  136.2 7.0 maximum_select_fusion.2
  155.4 6.5 maximum_select_fusion.1
  161.9 475.5 %collective-permute-done.2 = bf16[1,224,128,128]{3,2,1,0:T(8,128)(2,1)} collective-permute-done((bf16[1,224,128,128]{3,2,1,0:T(8,128)(2,1)}, bf16[1,224,128,128]{3,2,1,0:T(8,128)(2,1)}, u32[]{:S(2)}, u32[]{:S(2)}) %collective-permute-start.2) | collective-permute-done | bytes 7340064 | tf_op jit(solution)/shard_map/ppermute | solution.py:92
  637.4 13.7 maximum_select_fusion
  651.1 189.2 %while.61 = (s32[]{:T(128)}, f32[128,28,128]{2,1,0:T(8,128)}, s32[448]{0:T(512)S(1)}, s32[]{:T(128)}, bf16[448,128,128]{2,1,0:T(8,128)(2,1)}, /*index=5*/s32[448...) while((s32[]{:T(128)}, f32[128,28,128]{2,1,0:T(8,128)}, ...), condition=%wide.region_3.5_spmd.clone, body=%wide.region_2.4_spmd.clone.sunk | while | flops 196940544 | bytes 19928416 | solution.py:45
  840.3 192.6 %while.60 = (s32[]{:T(128)}, f32[128,28,128]{2,1,0:T(8,128)}, s32[448]{0:T(512)S(1)}, s32[]{:T(128)}, bf16[448,128,128]{2,1,0:T(8,128)(2,1)}, /*index=5*/s32[448...) while((s32[]{:T(128)}, f32[128,28,128]{2,1,0:T(8,128)}, ...), condition=%wide.region_1.3_spmd.clone, body=%wide.region_0.2_spmd.clone.sunk | while | flops 196940544 | bytes 19928416 | solution.py:45
  1032.9 6.5 multiply_convert_fusion.1
  1049.1 9.4 gather_fusion.5
  1058.5 9.2 gather_fusion.9
  1069.3 9.2 gather_fusion.7
  1082.3 9.1 gather_fusion.11
  1091.4 18.4 %fusion.105 = f32[224,128,128]{2,1,0:T(8,128)} fusion(bf16[224,256,128]{2,1,0:T(8,128)(2,1)} %gather_fusion.7, pred[224]{0:T(512)(128)(4,1)S(1)} %get-tuple-element.961, bf16[224,256,128]{2,1,0:T(8,128)(2,1)} %gather_fusion.5, pred[224]{0:T(512)(128)(4,1)S(1)} %get-tuple-element.963, f32[224]{0:T(256)S(1)} %get-tuple-element.960), kind=kOutput, calls=%fused_computation.142 | convolution fusion | flops 1897398272 | bytes 44041536 | tf_op jit(solution)/shard_map/tsk,tsn->skn/dot_general | solution.py:153
  1109.9 18.6 %fusion.110 = f32[224,128,128]{2,1,0:T(8,128)} fusion(bf16[224,256,128]{2,1,0:T(8,128)(2,1)} %gather_fusion.11, pred[224]{0:T(512)(128)(4,1)S(1)} %get-tuple-element.944, bf16[224,256,128]{2,1,0:T(8,128)(2,1)} %gather_fusion.9, pred[224]{0:T(512)(128)(4,1)S(1)} %get-tuple-element.941, f32[224]{0:T(256)S(1)} %get-tuple-element.959), kind=kOutput, calls=%fused_computation.143 | convolution fusion | flops 1897398272 | bytes 44041536 | tf_op jit(solution)/shard_map/tsk,tsn->skn/dot_general | solution.py:153
  1128.5 10.1 fusion.115
  1139.6 192.4 %while.62 = (s32[]{:T(128)}, f32[128,32,128]{2,1,0:T(8,128)}, s32[448]{0:T(512)S(1)}, s32[]{:T(128)}, bf16[448,128,128]{2,1,0:T(8,128)(2,1)}, /*index=5*/s32[448...) while((s32[]{:T(128)}, f32[128,32,128]{2,1,0:T(8,128)}, ...), condition=%wide.region_5.8_spmd.clone.clone, body=%wide.region_4.7_spmd.clone.clone.sunk | while | flops 205526272 | bytes 20976992 | solution.py:66
  1162.6 3.9 bitcast_add_fusion.10
  1176.4 3.9 bitcast_add_fusion.10
  1190.2 3.9 bitcast_add_fusion.10
  1204.0 3.9 bitcast_add_fusion.10
  1217.8 3.9 bitcast_add_fusion.10
  1231.6 3.9 bitcast_add_fusion.10
  1245.4 3.9 bitcast_add_fusion.10
  1259.2 3.9 bitcast_add_fusion.10
  1273.0 3.9 bitcast_add_fusion.10
  1286.8 3.9 bitcast_add_fusion.10
  1300.6 3.9 bitcast_add_fusion.10
  1314.4 3.9 bitcast_add_fusion.10
  1332.1 8.6 fusion.90
  1340.7 5.1 copy-done.7
  1351.9 186.2 %while.63 = (s32[]{:T(128)}, f32[128,32,128]{2,1,0:T(8,128)}, s32[448]{0:T(512)}, s32[]{:T(128)}, bf16[448,128,128]{2,1,0:T(8,128)(2,1)}, /*index=5*/s32[448]{0:...) while((s32[]{:T(128)}, f32[128,32,128]{2,1,0:T(8,128)}, ...), condition=%wide.region_7.10_spmd.clone.clone, body=%wide.region_6.9_spmd.clone.clone.sunk | while | flops 205526272 | bytes 24647044 | solution.py:66
  1374.0 3.9 bitcast_add_fusion.11
  1387.4 3.9 bitcast_add_fusion.11
  1400.7 3.9 bitcast_add_fusion.11
  1414.0 3.9 bitcast_add_fusion.11
  1427.4 3.9 bitcast_add_fusion.11
  1440.7 3.9 bitcast_add_fusion.11
  1454.1 3.9 bitcast_add_fusion.11
  1467.4 3.9 bitcast_add_fusion.11
  1480.8 3.9 bitcast_add_fusion.11
  1494.1 3.9 bitcast_add_fusion.11
  1507.5 3.9 bitcast_add_fusion.11
  1520.8 3.9 bitcast_add_fusion.11
  1534.2 3.9 bitcast_add_fusion.11
  1544.3 5.8 add_bitcast_fusion
  1553.0 12.5 reduce-scatter.2.cloned.1.call-done
  (583 shorter events, 711.1 us)
Async XLA Ops:
  7.2 144.3 %all-gather.5.cloned.1.call-start = ((), (), s32[]{:S(2)}) async-start(), calls=%async_computation.2 | async-start | bytes 1310720 | tf_op jit(solution)/shard_map/all_gather | solution.py:81
  7.2 43.4 %collective-permute-start = (bf16[1,56,128,128]{3,2,1,0:T(8,128)(2,1)}, bf16[1,56,128,128]{3,2,1,0:T(8,128)(2,1)}, u32[]{:S(2)}, u32[]{:S(2)}) collective-permute-start(bf16[1,56,128,128]{3,2,1,0:T(8,128)(2,1)} %param.31), channel_id=1, source_target_pairs={{0,4},{4,0},{8,12},{12,8},{16,20},{20,16},{24,28},{28,24},{1,5},{5... | collective-permute-start | bytes 5505032 | tf_op jit(solution)/shard_map/ppermute | solution.py:92
  10.2 46.9 %copy-start.12 = (bf16[128,1024]{1,0:T(8,128)(2,1)S(1)}, bf16[128,1024]{1,0:T(8,128)(2,1)}, u32[]{:S(2)}) copy-start(bf16[128,1024]{1,0:T(8,128)(2,1)} %param.28) | copy-start | bytes 786436
  10.2 47.8 %copy-start.9 = (bf16[1,56,128,128]{3,2,1,0:T(8,128)(2,1)S(1)}, bf16[1,56,128,128]{3,2,1,0:T(8,128)(2,1)}, u32[]{:S(2)}) copy-start(bf16[1,56,128,128]{3,2,1,0:T(8,128)(2,1)} %param.31) | copy-start | bytes 5505028
  55.3 80.8 %collective-permute-start.1 = (bf16[1,112,128,128]{3,2,1,0:T(8,128)(2,1)}, bf16[1,112,128,128]{3,2,1,0:T(8,128)(2,1)}, u32[]{:S(2)}, u32[]{:S(2)}) collective-permute-start(bf16[1,112,128,128]{3,2,1,0:T(8,128)(2,1)} %maximum_select_fusion.4), channel_id=1, source_target_pairs={{0,8},{4,12},{8,0},{12,4},{16,24},{20,28},{24,16},{28,20},{1,9},{5... | collective-permute-start | bytes 11010056 | tf_op jit(solution)/shard_map/ppermute | solution.py:92
  58.0 782.3 %all-gather.3.cloned.1.call-start = ((), (), s32[]{:S(2)}) async-start(), calls=%async_computation.1 | async-start | bytes 16515072 | tf_op jit(solution)/shard_map/all_gather | solution.py:86
  60.5 82.6 %copy-start.8 = (bf16[112,128,128]{2,1,0:T(8,128)(2,1)}, bf16[112,128,128]{2,1,0:T(8,128)(2,1)S(1)}, u32[]{:S(2)}) copy-start(bf16[112,128,128]{2,1,0:T(8,128)(2,1)S(1)} %maximum_select_fusion.3) | copy-start | bytes 11010052
  136.2 9.7 copy-start.11
  143.1 6.4 copy-start.3
  143.1 494.3 %collective-permute-start.2 = (bf16[1,224,128,128]{3,2,1,0:T(8,128)(2,1)}, bf16[1,224,128,128]{3,2,1,0:T(8,128)(2,1)}, u32[]{:S(2)}, u32[]{:S(2)}) collective-permute-start(bf16[1,224,128,128]{3,2,1,0:T(8,128)(2,1)} %maximum_select_fusion.2), channel_id=1, source_target_pairs={{0,16},{4,20},{8,24},{12,28},{16,0},{20,4},{24,8},{28,12},{1,17},{... | collective-permute-start | bytes 22020104 | tf_op jit(solution)/shard_map/ppermute | solution.py:92
  145.7 1419.8 %reduce-scatter.2.cloned.1.call-start = ((), (), s32[]{:S(2)}) async-start(), calls=%async_computation.3 | async-start | bytes 1310720 | tf_op jit(solution)/shard_map/reduce_scatter | solution.py:127
  153.9 893.6 %collective-permute-start.3 = (bf16[128,32,128]{2,0,1:T(8,128)(2,1)}, bf16[128,32,128]{2,0,1:T(8,128)(2,1)}, u32[]{:S(2)}, u32[]{:S(2)}) collective-permute-start(bf16[128,32,128]{2,0,1:T(8,128)(2,1)} %copy.98), channel_id=1, source_target_pairs={{0,4},{4,0},{8,12},{12,8},{16,20},{20,16},{24,28},{28,24},{1,5},{5... | collective-permute-start | bytes 3145736 | tf_op jit(solution)/shard_map/ppermute | solution.py:11
  637.4 13.7 copy-start.2
  651.1 189.2 %copy-start = (s32[1,448]{1,0:T(1,128)S(1)}, s32[1,448]{1,0:T(1,128)}, u32[]{:S(2)}) copy-start(s32[1,448]{1,0:T(1,128)} %param.33) | copy-start | bytes 5380
  651.1 189.2 %copy-start.1 = (s32[1,448]{1,0:T(1,128)S(1)}, s32[1,448]{1,0:T(1,128)}, u32[]{:S(2)}) copy-start(s32[1,448]{1,0:T(1,128)} %param.32) | copy-start | bytes 5380
  1039.4 41.6 %copy-start.4 = (bf16[128,28,128]{2,0,1:T(8,128)(2,1)}, bf16[128,28,128]{2,0,1:T(8,128)(2,1)S(1)}, u32[]{:S(2)}) copy-start(bf16[128,28,128]{2,0,1:T(8,128)(2,1)S(1)} %get-tuple-element.1284) | copy-start | bytes 2752516
  1039.4 28.4 %collective-permute-start.4 = (bf16[128,28,128]{2,0,1:T(8,128)(2,1)}, bf16[128,28,128]{2,0,1:T(8,128)(2,1)}, u32[]{:S(2)}, u32[]{:S(2)}) collective-permute-start(bf16[128,28,128]{2,0,1:T(8,128)(2,1)} %get-tuple-element.1251), channel_id=1, source_target_pairs={{0,4},{4,0},{8,12},{12,8},{16,20},{20,16},{24,28},{28,24},{1,5},{5... | collective-permute-start | bytes 2752520 | tf_op jit(solution)/shard_map/ppermute | solution.py:11
  1040.6 40.4 %collective-permute-start.5 = (bf16[128,28,128]{2,0,1:T(8,128)(2,1)S(1)}, bf16[128,28,128]{2,0,1:T(8,128)(2,1)}, u32[]{:S(2)}, u32[]{:S(2)}) collective-permute-start(bf16[128,28,128]{2,0,1:T(8,128)(2,1)S(1)} %get-tuple-element.1284), channel_id=1, source_target_pairs={{0,4},{4,0},{8,12},{12,8},{16,20},{20,16},{24,28},{28,24},{1,5},{5... | collective-permute-start | bytes 2752520 | tf_op jit(solution)/shard_map/ppermute | solution.py:11
  1138.6 193.5 %collective-permute-start.6 = (bf16[2,56,2,128,128]{4,3,1,2,0:T(8,128)(2,1)}, bf16[2,56,2,128,128]{4,3,1,2,0:T(8,128)(2,1)}, u32[]{:S(2)}, u32[]{:S(2)}) collective-permute-start(bf16[2,56,2,128,128]{4,3,1,2,0:T(8,128)(2,1)} %fusion.115), channel_id=1, source_target_pairs={{0,8},{4,12},{8,0},{12,4},{16,24},{20,28},{24,16},{28,20},{1,9},{5... | collective-permute-start | bytes 22020104 | tf_op jit(solution)/shard_map/ppermute | solution.py:11
  1340.7 5.2 copy-start.7
  1345.8 6.1 copy-start.5
  1348.6 195.8 %collective-permute-start.7 = (bf16[1,56,2,128,128]{4,3,1,2,0:T(8,128)(2,1)}, bf16[1,56,2,128,128]{4,3,1,2,0:T(8,128)(2,1)}, u32[]{:S(2)}, u32[]{:S(2)}) collective-permute-start(bf16[1,56,2,128,128]{4,3,1,2,0:T(8,128)(2,1)} %dynamic-slice_convert_fusion), channel_id=1, source_target_pairs={{0,16},{4,20},{8,24},{12,28},{16,0},{20,4},{24,8},{28,12},{1,17},{... | collective-permute-start | bytes 11010056 | tf_op jit(solution)/shard_map/ppermute | solution.py:11
  1361.3 3.3 copy-start.6
  1374.0 3.9 copy-start.6
  1387.4 3.9 copy-start.6
  1400.7 3.9 copy-start.6
  1414.0 3.9 copy-start.6
  1427.4 3.9 copy-start.6
  1440.7 3.9 copy-start.6
  1454.1 3.9 copy-start.6
  1467.4 3.9 copy-start.6
  1480.8 3.9 copy-start.6
  1494.1 3.9 copy-start.6
  1507.5 3.9 copy-start.6
  1520.8 3.9 copy-start.6
  1534.2 3.9 copy-start.6
  1538.1 4.3 copy-start.10
Sparse Core Ops, SparseCore 0:
  58.2 16.9 all-gather.4
  145.8 432.7 all-gather.2
  1542.5 22.9 reduce-scatter.1
